TPU v7x, 128 devices: a whole 4x4x4 slice. The times are simulated.
128 devices in a mesh: fsdp: 16 (over z_lo, y, core), tp: 8 (over x, z_hi).
Axes of the slice: x: 4, y: 4, z: 4 (z_hi: 2, z_lo: 2; z = z_hi * 2 + z_lo), core: 2. Of those that a mesh axis runs over, the one named last changes fastest.
Arguments:
- probe_states: bfloat16 [256, 16384], P('fsdp'), may hold values from -6 to 6
- wq_master: float32 [16384, 4096], P(('fsdp', 'tp')), may hold values from -1 to 1
- wq_first: float32 [16384, 4096], P(('fsdp', 'tp')), may hold values from -6 to 6
- wq_second: float32 [16384, 4096], P(('fsdp', 'tp')), may hold values from 0.25 to 4
- wq_grad: float32 [16384, 4096], P('fsdp', 'tp'), may hold values from -6 to 6
- wkv_master: float32 [16384, 512], P(('fsdp', 'tp')), may hold values from -0.046875 to 0.046875
- wkv_first: float32 [16384, 512], P(('fsdp', 'tp')), may hold values from -6 to 6
- wkv_second: float32 [16384, 512], P(('fsdp', 'tp')), may hold values from 0.25 to 4
- wkv_grad: float32 [16384, 512], P(('fsdp', 'tp')), may hold values from -6 to 6
Outputs:
- wq_updated: float32 [16384, 4096], P('fsdp', 'tp')
- wq_first_new: float32 [16384, 4096], P('fsdp', 'tp')
- wq_second_new: float32 [16384, 4096], P('fsdp', 'tp')
- wkv_updated: float32 [16384, 512], P(('fsdp', 'tp'))
- wkv_first_new: float32 [16384, 512], P(('fsdp', 'tp'))
- wkv_second_new: float32 [16384, 512], P(('fsdp', 'tp'))
- probe_query: bfloat16 [256, 4096], P('fsdp', 'tp')
- probe_keyvalue: bfloat16 [256, 512], replicated
All inputs are finite; a program needn't handle non-finite values.
Results may differ from a plain program's by a relative error of at most 0.008.
Values may be sent and summed in bfloat16 or wider, within the bound.
A program may use at most 128 MiB of HBM per device.

v0:
```python
import math
import jax
import jax.numpy as jnp
from jax import lax
from jax.sharding import PartitionSpec as P

BETA_ONE = 0.9
BETA_TWO = 0.95
LEARN_RATE = 0.001
EPSILON = 1e-08
CORRECT_ONE = 1.0 - math.exp(1000.0 * math.log(0.9))
CORRECT_TWO = 1.0 - math.exp(1000.0 * math.log(0.95))


def adam_step(master, first, second, grad):
    first_new = BETA_ONE * first + (1.0 - BETA_ONE) * grad
    second_new = BETA_TWO * second + (1.0 - BETA_TWO) * grad * grad
    update = first_new / CORRECT_ONE / (jnp.sqrt(second_new / CORRECT_TWO) + EPSILON)
    return (master - LEARN_RATE * update, first_new, second_new)


def body(
    probe_states,
    wq_master,
    wq_first,
    wq_second,
    wq_grad,
    wkv_master,
    wkv_first,
    wkv_second,
    wkv_grad,
):
    master, first, second = (
        lax.all_to_all(wq_master, "tp", split_axis=1, concat_axis=0, tiled=True),
        lax.all_to_all(wq_first, "tp", split_axis=1, concat_axis=0, tiled=True),
        lax.all_to_all(wq_second, "tp", split_axis=1, concat_axis=0, tiled=True),
    )
    wq_new, wq_mom, wq_var = adam_step(master, first, second, wq_grad)
    wkv_new, wkv_mom, wkv_var = adam_step(wkv_master, wkv_first, wkv_second, wkv_grad)
    columns = lax.all_to_all(probe_states, "fsdp", split_axis=1, concat_axis=0, tiled=True)
    tp_rank = lax.axis_index("tp")
    kv_rows = wkv_master.shape[0]
    own_columns = lax.dynamic_slice_in_dim(columns, tp_rank * kv_rows, kv_rows, 1)
    kv_term = jnp.dot(own_columns, wkv_new.astype(jnp.bfloat16), preferred_element_type=jnp.float32)
    probe_keyvalue = lax.psum(kv_term, ("fsdp", "tp")).astype(jnp.bfloat16)
    wq_low = wq_new.astype(jnp.bfloat16)
    queries = jnp.dot(
        probe_states,
        lax.all_gather(wq_low, "fsdp", axis=0, tiled=True),
        preferred_element_type=jnp.float32,
    )
    probe_query = queries.astype(jnp.bfloat16)
    return (wq_new, wq_mom, wq_var, wkv_new, wkv_mom, wkv_var, probe_query, probe_keyvalue)


def solution(mesh):
    return jax.shard_map(
        body,
        mesh=mesh,
        in_specs=(
            P("fsdp", None),
            P(("fsdp", "tp"), None),
            P(("fsdp", "tp"), None),
            P(("fsdp", "tp"), None),
            P("fsdp", "tp"),
            P(("fsdp", "tp"), None),
            P(("fsdp", "tp"), None),
            P(("fsdp", "tp"), None),
            P(("fsdp", "tp"), None),
        ),
        out_specs=(
            P("fsdp", "tp"),
            P("fsdp", "tp"),
            P("fsdp", "tp"),
            P(("fsdp", "tp"), None),
            P(("fsdp", "tp"), None),
            P(("fsdp", "tp"), None),
            P("fsdp", "tp"),
            P(),
        ),
        check_vma=False,
    )
```

profile of v0, /device:TPU:1, one launch (start us, length us, event | category | flops | bytes accessed | tf_op | source)
XLA Modules:
  0.0 238.8 jit_solution(16143131540047762686)
XLA Ops:
  7.2 3.1 %copy.39 = f32[16,8,8,512]{3,2,0,1:T(8,128)} copy(f32[16,8,8,512]{3,2,1,0:T(8,128)} %bitcast.42) | data formatting | bytes 4194304 | tf_op jit(solution)/shard_map/all_to_all | solution.py:36
  10.3 8.2 %all-to-all-start.2 = ((f32[128,8,512]{2,0,1:T(8,128)}), f32[128,8,512]{2,0,1:T(8,128)S(1)}, u32[]{:S(2)}, u32[]{:S(2)}) async-start(f32[128,8,512]{2,0,1:T(8,128)} %bitcast.40), calls=%async_computation.2 | async-start | bytes 4194304 | tf_op jit(solution)/shard_map/all_to_all | solution.py:36
  18.5 3.1 %copy.40 = f32[16,8,8,512]{3,2,0,1:T(8,128)} copy(f32[16,8,8,512]{3,2,1,0:T(8,128)} %bitcast.43) | data formatting | bytes 4194304 | tf_op jit(solution)/shard_map/all_to_all | solution.py:35
  21.6 27.5 %all-to-all-done.2 = f32[128,8,512]{2,0,1:T(8,128)S(1)} async-done(((f32[128,8,512]{2,0,1:T(8,128)}), f32[128,8,512]{2,0,1:T(8,128)S(1)}, u32[]{:S(2)}, u32[]{:S(2)}) %all-to-all-start.2) | async-done | bytes 2097184 | tf_op jit(solution)/shard_map/all_to_all | solution.py:36
  49.1 0.0 copy-start
  49.1 1.3 copy-done
  50.4 4.4 %all-to-all-start.1 = ((f32[128,8,512]{2,0,1:T(8,128)}), f32[128,8,512]{2,0,1:T(8,128)}, u32[]{:S(2)}, u32[]{:S(2)}) async-start(f32[128,8,512]{2,0,1:T(8,128)} %bitcast.39), calls=%async_computation.1 | async-start | bytes 4194304 | tf_op jit(solution)/shard_map/all_to_all | solution.py:35
  54.8 3.2 %copy.41 = f32[16,8,8,512]{3,2,0,1:T(8,128)} copy(f32[16,8,8,512]{3,2,1,0:T(8,128)} %bitcast.44) | data formatting | bytes 4194304 | tf_op jit(solution)/shard_map/all_to_all | solution.py:34
  57.9 26.7 %all-to-all-done.1 = f32[128,8,512]{2,0,1:T(8,128)} async-done(((f32[128,8,512]{2,0,1:T(8,128)}), f32[128,8,512]{2,0,1:T(8,128)}, u32[]{:S(2)}, u32[]{:S(2)}) %all-to-all-start.1) | async-done | bytes 2097184 | tf_op jit(solution)/shard_map/all_to_all | solution.py:35
  84.6 3.6 %all-to-all-start = ((f32[128,8,512]{2,0,1:T(8,128)}), f32[128,8,512]{2,0,1:T(8,128)S(1)}, u32[]{:S(2)}, u32[]{:S(2)}) async-start(f32[128,8,512]{2,0,1:T(8,128)} %bitcast.38), calls=%async_computation | async-start | bytes 4194304 | tf_op jit(solution)/shard_map/all_to_all | solution.py:34
  88.2 0.0 all-gather.2.cloned.1.call-start
  88.2 3.3 %broadcast_multiply_fusion = f32[128,8,512]{2,0,1:T(8,128)} fusion(f32[128,8,512]{2,0,1:T(8,128)} %copy-done), kind=kLoop, calls=%fused_computation.9 | loop fusion | flops 524288 | bytes 4194304 | tf_op jit(solution)/shard_map/mul | solution.py:17
  91.5 3.3 %broadcast_multiply_fusion.1 = f32[128,8,512]{2,0,1:T(8,128)} fusion(f32[128,8,512]{2,0,1:T(8,128)} %all-to-all-done.1), kind=kLoop, calls=%fused_computation.10 | loop fusion | flops 524288 | bytes 4194304 | tf_op jit(solution)/shard_map/mul | solution.py:16
  94.8 0.0 copy-start.1
  94.8 22.8 %all-to-all-done = f32[128,8,512]{2,0,1:T(8,128)S(1)} async-done(((f32[128,8,512]{2,0,1:T(8,128)}), f32[128,8,512]{2,0,1:T(8,128)S(1)}, u32[]{:S(2)}, u32[]{:S(2)}) %all-to-all-start) | async-done | bytes 2097184 | tf_op jit(solution)/shard_map/all_to_all | solution.py:34
  117.5 6.7 %fusion.7 = (bf16[1024,512]{1,0:T(8,128)(2,1)}, f32[1024,512]{1,0:T(8,128)}, f32[1024,512]{1,0:T(8,128)}, f32[1024,512]{1,0:T(8,128)}) fusion(f32[128,8,512]{2,0,1:T(8,128)S(1)} %all-to-all-done, f32[1024,512]{1,0:T(8,128)} %param.13, f32[128,8,512]{2,0,1:T(8,128)} %broadcast_multiply_fusion, f32[128,8,512]{2,0,1:T(8,128)} %broadcast_multiply_fusion.1), kind=kLoop, calls=%fused_computation.20 | loop fusion | flops 5242880 | bytes 15728640 | tf_op jit(solution)/shard_map/convert_element_type | solution.py:46
  124.3 0.0 copy-start.6
  124.3 0.0 all-gather.2.cloned.1.call-update
  124.3 0.0 copy-done.1
  124.3 0.9 copy.42
  125.2 7.0 %all-to-all-start.3 = ((bf16[16,16,1024]{2,0,1:T(8,128)(2,1)}), bf16[16,16,1024]{2,0,1:T(8,128)(2,1)S(1)}, u32[]{:S(2)}, u32[]{:S(2)}) async-start(bf16[16,16,1024]{2,0,1:T(8,128)(2,1)} %bitcast.37), calls=%async_computation.3 | async-start | bytes 1048576 | tf_op jit(solution)/shard_map/all_to_all | solution.py:40
  132.2 0.0 copy-done.3
  132.2 0.0 copy-done.4
  132.2 0.0 copy-done.5
  132.2 0.0 copy-done.6
  132.2 0.9 multiply_subtract_fusion
  133.2 13.5 %all-to-all-done.3 = bf16[16,16,1024]{2,0,1:T(8,128)(2,1)S(1)} async-done(((bf16[16,16,1024]{2,0,1:T(8,128)(2,1)}), bf16[16,16,1024]{2,0,1:T(8,128)(2,1)S(1)}, u32[]{:S(2)}, u32[]{:S(2)}) %all-to-all-start.3) | async-done | bytes 524320 | tf_op jit(solution)/shard_map/all_to_all | solution.py:40
  146.6 0.2 fusion.3
  146.8 68.1 %all-reduce.1 = bf16[256,512]{1,0:T(8,128)(2,1)} all-reduce(f32[256,512]{1,0:T(8,128)S(1)} %fusion.3), channel_id=1, replica_groups=mesh['fsdp'=16,'tp'=8] {'fsdp','tp'}, use_global_device_ids=true, to_apply=%region_0.0 | all-reduce | flops 131072 | bytes 786432 | tf_op jit(solution)/shard_map/psum | solution.py:45
  214.9 8.3 %all-gather.2.cloned.1.call-done = bf16[16384,512]{1,0:T(8,128)(2,1)} async-done(((bf16[1024,512]{1,0:T(8,128)(2,1)}), bf16[16384,512]{1,0:T(8,128)(2,1)}) %all-gather.2.cloned.1.call-update) | async-done | bytes 16777232 | tf_op jit(solution)/shard_map/all_gather | solution.py:49
  223.3 8.6 %fusion.1 = bf16[16,512]{1,0:T(8,128)(2,1)} fusion(bf16[16,16384]{1,0:T(8,128)(2,1)S(1)} %copy-done.1, bf16[16384,512]{1,0:T(8,128)(2,1)} %all-gather.2.cloned.1.call-done), kind=kOutput, calls=%fused_computation.8 | convolution fusion | flops 268443648 | bytes 17317888 | tf_op jit(solution)/shard_map/dot_general | solution.py:47
  231.9 0.0 copy-done.2
  (4 shorter events, 0.0 us)
Async XLA Ops:
  10.3 38.8 %all-to-all-start.2 = ((f32[128,8,512]{2,0,1:T(8,128)}), f32[128,8,512]{2,0,1:T(8,128)S(1)}, u32[]{:S(2)}, u32[]{:S(2)}) async-start(f32[128,8,512]{2,0,1:T(8,128)} %bitcast.40), calls=%async_computation.2 | async-start | bytes 4194304 | tf_op jit(solution)/shard_map/all_to_all | solution.py:36
  49.1 1.3 copy-start
  50.4 34.2 %all-to-all-start.1 = ((f32[128,8,512]{2,0,1:T(8,128)}), f32[128,8,512]{2,0,1:T(8,128)}, u32[]{:S(2)}, u32[]{:S(2)}) async-start(f32[128,8,512]{2,0,1:T(8,128)} %bitcast.39), calls=%async_computation.1 | async-start | bytes 4194304 | tf_op jit(solution)/shard_map/all_to_all | solution.py:35
  84.6 33.0 %all-to-all-start = ((f32[128,8,512]{2,0,1:T(8,128)}), f32[128,8,512]{2,0,1:T(8,128)S(1)}, u32[]{:S(2)}, u32[]{:S(2)}) async-start(f32[128,8,512]{2,0,1:T(8,128)} %bitcast.38), calls=%async_computation | async-start | bytes 4194304 | tf_op jit(solution)/shard_map/all_to_all | solution.py:34
  88.2 135.1 %all-gather.2.cloned.1.call-start = ((), (), s32[]{:S(2)}) async-start(), calls=%async_computation.4 | async-start | bytes 17825792 | tf_op jit(solution)/shard_map/all_gather | solution.py:49
  94.8 29.5 %copy-start.1 = (bf16[16,16384]{1,0:T(8,128)(2,1)S(1)}, bf16[16,16384]{1,0:T(8,128)(2,1)}, u32[]{:S(2)}) copy-start(bf16[16,16384]{1,0:T(8,128)(2,1)} %param.9) | copy-start | bytes 1572868
  124.3 7.9 %copy-start.3 = (f32[128,512]{1,0:T(8,128)S(1)}, f32[128,512]{1,0:T(8,128)}, u32[]{:S(2)}) copy-start(f32[128,512]{1,0:T(8,128)} %param.14) | copy-start | bytes 786436
  124.3 7.9 %copy-start.4 = (f32[128,512]{1,0:T(8,128)S(1)}, f32[128,512]{1,0:T(8,128)}, u32[]{:S(2)}) copy-start(f32[128,512]{1,0:T(8,128)} %param.17) | copy-start | bytes 786436
  124.3 7.9 %copy-start.5 = (f32[128,512]{1,0:T(8,128)S(1)}, f32[128,512]{1,0:T(8,128)}, u32[]{:S(2)}) copy-start(f32[128,512]{1,0:T(8,128)} %param.16) | copy-start | bytes 786436
  124.3 7.9 %copy-start.6 = (f32[128,512]{1,0:T(8,128)S(1)}, f32[128,512]{1,0:T(8,128)}, u32[]{:S(2)}) copy-start(f32[128,512]{1,0:T(8,128)} %param.15) | copy-start | bytes 786436
  125.2 21.4 %all-to-all-start.3 = ((bf16[16,16,1024]{2,0,1:T(8,128)(2,1)}), bf16[16,16,1024]{2,0,1:T(8,128)(2,1)S(1)}, u32[]{:S(2)}, u32[]{:S(2)}) async-start(bf16[16,16,1024]{2,0,1:T(8,128)(2,1)} %bitcast.37), calls=%async_computation.3 | async-start | bytes 1048576 | tf_op jit(solution)/shard_map/all_to_all | solution.py:40
  133.1 98.8 %copy-start.2 = (f32[128,512]{1,0:T(8,128)}, f32[128,512]{1,0:T(8,128)S(1)}, u32[]{:S(2)}) copy-start(f32[128,512]{1,0:T(8,128)S(1)} %get-tuple-element.12) | copy-start | bytes 786436
Sparse Core Ops, SparseCore 0:
  124.5 98.7 all-gather.1
where the time goes:
time: 239 us
  waiting for transfers between devices  98.7 us (41%)
  blocking collectives  68.1 us (28%)
  starting transfers between devices  23.1 us (10%)
  other arithmetic  14.3 us (6%)
  between operations  14.1 us (6%)
  local copies, waits for them, and re-layouts  11.7 us (5%)
  matrix products  8.86 us (4%)
    psum x1, blocking collectives, body(): probe_keyvalue = lax.psum(kv_term, ('fsdp', 'tp')).astype(jnp.bfloat16)  68.1 us
    all_to_all x1, waiting for transfers between devices, body(): lax.all_to_all(wq_second, 'tp', split_axis=1, concat_axis=0, tiled=True)  27.5 us
    all_to_all x1, waiting for transfers between devices, body(): lax.all_to_all(wq_first, 'tp', split_axis=1, concat_axis=0, tiled=True)  26.7 us
    all_to_all x1, waiting for transfers between devices, body(): lax.all_to_all(wq_master, 'tp', split_axis=1, concat_axis=0, tiled=True)  22.8 us
    all_to_all x1, waiting for transfers between devices, body(): lax.all_to_all(probe_states, 'fsdp', split_axis=1, concat_axis=0, tiled=T...  13.5 us
    dot_general x1, matrix products, body(): jnp.dot(probe_states, lax.all_gather(wq_low, 'fsdp', axis=0, tiled=True),...  8.65 us
    all_gather x1, waiting for transfers between devices, body(): lax.all_gather(wq_low, 'fsdp', axis=0, tiled=True)  8.34 us
    all_to_all x1, starting transfers between devices, body(): lax.all_to_all(wq_second, 'tp', split_axis=1, concat_axis=0, tiled=True)  8.15 us
  transfers between devices with their start and end apart: 5, of which 5 were waited for; matrix products, arithmetic and copies ran while one was open for 6% of the time, Pallas kernels for 0%

commit v1 on v0

--- a/solution.py
+++ b/solution.py
@@ -1,3 +1,4 @@
+import functools
 import math
 import jax
 import jax.numpy as jnp
@@ -10,6 +11,13 @@
 EPSILON = 1e-08
 CORRECT_ONE = 1.0 - math.exp(1000.0 * math.log(0.9))
 CORRECT_TWO = 1.0 - math.exp(1000.0 * math.log(0.95))
+
+
+def watch_pipes(buf, mesh_name):
+    return lax.all_gather(buf, mesh_name).sum(axis=0)
+
+
+group_roots_by_axis = functools.partial(watch_pipes, mesh_name=("fsdp", "tp"))
 
 
 def adam_step(master, first, second, grad):
@@ -42,7 +50,7 @@
     kv_rows = wkv_master.shape[0]
     own_columns = lax.dynamic_slice_in_dim(columns, tp_rank * kv_rows, kv_rows, 1)
     kv_term = jnp.dot(own_columns, wkv_new.astype(jnp.bfloat16), preferred_element_type=jnp.float32)
-    probe_keyvalue = lax.psum(kv_term, ("fsdp", "tp")).astype(jnp.bfloat16)
+    probe_keyvalue = group_roots_by_axis(kv_term).astype(jnp.bfloat16)
     wq_low = wq_new.astype(jnp.bfloat16)
     queries = jnp.dot(
         probe_states,

time: 239 us -> 632 us (2.64)
  waiting for transfers between devices: 98.7 us -> 537 us
  blocking collectives: 68.1 us -> 0 us
  other arithmetic: 14.3 us -> 35.8 us
    all_gather x0 -> x1, waiting for transfers between devices: none -> 374 us  [watch_pipes(): return lax.all_gather(buf, mesh_name).sum(axis=0)]
    psum x1 -> x0, blocking collectives: 68.1 us -> none  [body(): probe_keyvalue = lax.psum(kv_term, ('fsdp', 'tp')).astype(jnp.bfloat16)]
    all_gather x1, waiting for transfers between devices: 8.34 us -> 72.7 us  [body(): lax.all_gather(wq_low, 'fsdp', axis=0, tiled=True)]
    reduce_sum x0 -> x1, other arithmetic: none -> 21.6 us  [watch_pipes(): return lax.all_gather(buf, mesh_name).sum(axis=0)]
  transfers between devices with their start and end apart: 5 -> 6, of which waited for: 5 -> 6; matrix products, arithmetic and copies ran while one was open for 6% -> 4% of each run, Pallas kernels for 0% -> 0%
where the time goes in v1:
time: 632 us; the launch traced here: 631 us
  waiting for transfers between devices  537 us (85%)
  other arithmetic  35.8 us (6%)
  starting transfers between devices  23.2 us (4%)
  between operations  14.1 us (2%)
  local copies, waits for them, and re-layouts  11.6 us (2%)
  matrix products  9.68 us (2%)
    all_gather x1, waiting for transfers between devices, watch_pipes(): return lax.all_gather(buf, mesh_name).sum(axis=0)  374 us
    all_gather x1, waiting for transfers between devices, body(): lax.all_gather(wq_low, 'fsdp', axis=0, tiled=True)  72.7 us
    all_to_all x1, waiting for transfers between devices, body(): lax.all_to_all(wq_first, 'tp', split_axis=1, concat_axis=0, tiled=True)  27.5 us
    all_to_all x1, waiting for transfers between devices, body(): lax.all_to_all(wq_second, 'tp', split_axis=1, concat_axis=0, tiled=True)  26.7 us
    all_to_all x1, waiting for transfers between devices, body(): lax.all_to_all(wq_master, 'tp', split_axis=1, concat_axis=0, tiled=True)  22.8 us
    reduce_sum x1, other arithmetic, watch_pipes(): return lax.all_gather(buf, mesh_name).sum(axis=0)  21.6 us
    all_to_all x1, waiting for transfers between devices, body(): lax.all_to_all(probe_states, 'fsdp', split_axis=1, concat_axis=0, tiled=T...  13.4 us
  transfers between devices with their start and end apart: 6, of which 6 were waited for; matrix products, arithmetic and copies ran while one was open for 4% of the time, Pallas kernels for 0%

profile of v1, /device:TPU:1, one launch (start us, length us, event | category | flops | bytes accessed | tf_op | source)
XLA Modules:
  0.0 631.3 jit_solution(15751688524574744290)
XLA Ops:
  7.2 3.1 copy.40
  10.3 8.2 %all-to-all-start.1 = ((f32[128,8,512]{2,0,1:T(8,128)}), f32[128,8,512]{2,0,1:T(8,128)S(1)}, u32[]{:S(2)}, u32[]{:S(2)}) async-start(f32[128,8,512]{2,0,1:T(8,128)} %bitcast.41), calls=%async_computation.1 | async-start | bytes 4194304 | tf_op jit(solution)/shard_map/all_to_all | solution.py:43
  18.5 3.1 copy.39
  21.6 27.5 %all-to-all-done.1 = f32[128,8,512]{2,0,1:T(8,128)S(1)} async-done(((f32[128,8,512]{2,0,1:T(8,128)}), f32[128,8,512]{2,0,1:T(8,128)S(1)}, u32[]{:S(2)}, u32[]{:S(2)}) %all-to-all-start.1) | async-done | bytes 2097184 | tf_op jit(solution)/shard_map/all_to_all | solution.py:43
  49.1 1.3 copy-done
  50.4 4.4 all-to-all-start.2
  54.8 3.2 copy.41
  57.9 26.7 %all-to-all-done.2 = f32[128,8,512]{2,0,1:T(8,128)} async-done(((f32[128,8,512]{2,0,1:T(8,128)}), f32[128,8,512]{2,0,1:T(8,128)}, u32[]{:S(2)}, u32[]{:S(2)}) %all-to-all-start.2) | async-done | bytes 2097184 | tf_op jit(solution)/shard_map/all_to_all | solution.py:44
  84.6 3.6 all-to-all-start
  88.2 0.0 all-gather.4.cloned.1.call-start
  88.3 3.3 broadcast_multiply_fusion.1
  91.5 3.3 broadcast_multiply_fusion
  94.8 22.8 %all-to-all-done = f32[128,8,512]{2,0,1:T(8,128)S(1)} async-done(((f32[128,8,512]{2,0,1:T(8,128)}), f32[128,8,512]{2,0,1:T(8,128)S(1)}, u32[]{:S(2)}, u32[]{:S(2)}) %all-to-all-start) | async-done | bytes 2097184 | tf_op jit(solution)/shard_map/all_to_all | solution.py:42
  117.6 6.7 %fusion.7 = (bf16[1024,512]{1,0:T(8,128)(2,1)}, f32[1024,512]{1,0:T(8,128)}, f32[1024,512]{1,0:T(8,128)}, f32[1024,512]{1,0:T(8,128)}) fusion(f32[128,8,512]{2,0,1:T(8,128)S(1)} %all-to-all-done, f32[1024,512]{1,0:T(8,128)} %param.13, f32[128,8,512]{2,0,1:T(8,128)} %broadcast_multiply_fusion, f32[128,8,512]{2,0,1:T(8,128)} %broadcast_multiply_fusion.1), kind=kLoop, calls=%fused_computation.20 | loop fusion | flops 5242880 | bytes 15728640 | tf_op jit(solution)/shard_map/convert_element_type | solution.py:54
  124.3 0.0 copy-start.6
  124.3 0.0 all-gather.4.cloned.1.call-update
  124.4 0.0 copy-done.1
  124.4 0.8 copy.42
  125.2 7.0 %all-to-all-start.3 = ((bf16[16,16,1024]{2,0,1:T(8,128)(2,1)}), bf16[16,16,1024]{2,0,1:T(8,128)(2,1)S(1)}, u32[]{:S(2)}, u32[]{:S(2)}) async-start(bf16[16,16,1024]{2,0,1:T(8,128)(2,1)} %bitcast.38), calls=%async_computation.3 | async-start | bytes 1048576 | tf_op jit(solution)/shard_map/all_to_all | solution.py:48
  132.1 0.0 all-gather.6.cloned.1.call-start
  132.2 0.0 copy-done.3
  132.2 0.0 copy-done.4
  132.2 0.0 copy-done.5
  132.2 0.9 multiply_subtract_fusion
  133.2 13.4 %all-to-all-done.3 = bf16[16,16,1024]{2,0,1:T(8,128)(2,1)S(1)} async-done(((bf16[16,16,1024]{2,0,1:T(8,128)(2,1)}), bf16[16,16,1024]{2,0,1:T(8,128)(2,1)S(1)}, u32[]{:S(2)}, u32[]{:S(2)}) %all-to-all-start.3) | async-done | bytes 524320 | tf_op jit(solution)/shard_map/all_to_all | solution.py:48
  146.6 1.0 fusion.3
  147.6 0.0 all-gather.6.cloned.1.call-update
  147.7 72.7 %all-gather.4.cloned.1.call-done = bf16[16384,512]{1,0:T(8,128)(2,1)} async-done(((bf16[1024,512]{1,0:T(8,128)(2,1)}), bf16[16384,512]{1,0:T(8,128)(2,1)}) %all-gather.4.cloned.1.call-update) | async-done | bytes 16777232 | tf_op jit(solution)/shard_map/all_gather | solution.py:57
  220.4 8.6 %fusion.1 = bf16[16,512]{1,0:T(8,128)(2,1)} fusion(bf16[16,16384]{1,0:T(8,128)(2,1)S(1)} %copy-done.1, bf16[16384,512]{1,0:T(8,128)(2,1)} %all-gather.4.cloned.1.call-done), kind=kOutput, calls=%fused_computation.8 | convolution fusion | flops 268443648 | bytes 17317888 | tf_op jit(solution)/shard_map/dot_general | solution.py:55
  229.0 0.0 copy-done.2
  229.0 373.8 %all-gather.6.cloned.1.call-done = f32[32768,512]{1,0:T(8,128)} async-done(((f32[256,512]{1,0:T(8,128)}), f32[32768,512]{1,0:T(8,128)}) %all-gather.6.cloned.1.call-update) | async-done | bytes 67108880 | tf_op jit(solution)/shard_map/all_gather | solution.py:17
  602.8 21.6 %reduce_sum.9 = bf16[256,512]{1,0:T(8,128)(2,1)} reduce(f32[128,256,512]{2,1,0:T(8,128)} %bitcast.9, f32[]{:T(128)} %constant.2.clone.1), dimensions={0}, to_apply=%region_0.0 | reduce | flops 16646144 | bytes 67371008 | tf_op jit(solution)/shard_map/reduce_sum | solution.py:17
  (7 shorter events, 0.0 us)
Async XLA Ops:
  10.3 38.8 %all-to-all-start.1 = ((f32[128,8,512]{2,0,1:T(8,128)}), f32[128,8,512]{2,0,1:T(8,128)S(1)}, u32[]{:S(2)}, u32[]{:S(2)}) async-start(f32[128,8,512]{2,0,1:T(8,128)} %bitcast.41), calls=%async_computation.1 | async-start | bytes 4194304 | tf_op jit(solution)/shard_map/all_to_all | solution.py:43
  49.1 1.3 copy-start
  50.4 34.2 %all-to-all-start.2 = ((f32[128,8,512]{2,0,1:T(8,128)}), f32[128,8,512]{2,0,1:T(8,128)}, u32[]{:S(2)}, u32[]{:S(2)}) async-start(f32[128,8,512]{2,0,1:T(8,128)} %bitcast.40), calls=%async_computation.2 | async-start | bytes 4194304 | tf_op jit(solution)/shard_map/all_to_all | solution.py:44
  84.6 33.0 %all-to-all-start = ((f32[128,8,512]{2,0,1:T(8,128)}), f32[128,8,512]{2,0,1:T(8,128)S(1)}, u32[]{:S(2)}, u32[]{:S(2)}) async-start(f32[128,8,512]{2,0,1:T(8,128)} %bitcast.39), calls=%async_computation | async-start | bytes 4194304 | tf_op jit(solution)/shard_map/all_to_all | solution.py:42
  88.2 132.2 %all-gather.4.cloned.1.call-start = ((), (), s32[]{:S(2)}) async-start(), calls=%async_computation.4 | async-start | bytes 17825792 | tf_op jit(solution)/shard_map/all_gather | solution.py:57
  94.8 29.6 %copy-start.1 = (bf16[16,16384]{1,0:T(8,128)(2,1)S(1)}, bf16[16,16384]{1,0:T(8,128)(2,1)}, u32[]{:S(2)}) copy-start(bf16[16,16384]{1,0:T(8,128)(2,1)} %param.9) | copy-start | bytes 1572868
  124.3 7.9 %copy-start.3 = (f32[128,512]{1,0:T(8,128)S(1)}, f32[128,512]{1,0:T(8,128)}, u32[]{:S(2)}) copy-start(f32[128,512]{1,0:T(8,128)} %param.14) | copy-start | bytes 786436
  124.3 7.9 %copy-start.4 = (f32[128,512]{1,0:T(8,128)S(1)}, f32[128,512]{1,0:T(8,128)}, u32[]{:S(2)}) copy-start(f32[128,512]{1,0:T(8,128)} %param.17) | copy-start | bytes 786436
  124.3 7.9 %copy-start.5 = (f32[128,512]{1,0:T(8,128)S(1)}, f32[128,512]{1,0:T(8,128)}, u32[]{:S(2)}) copy-start(f32[128,512]{1,0:T(8,128)} %param.16) | copy-start | bytes 786436
  124.3 7.9 %copy-start.6 = (f32[128,512]{1,0:T(8,128)S(1)}, f32[128,512]{1,0:T(8,128)}, u32[]{:S(2)}) copy-start(f32[128,512]{1,0:T(8,128)} %param.15) | copy-start | bytes 786436
  125.2 21.4 %all-to-all-start.3 = ((bf16[16,16,1024]{2,0,1:T(8,128)(2,1)}), bf16[16,16,1024]{2,0,1:T(8,128)(2,1)S(1)}, u32[]{:S(2)}, u32[]{:S(2)}) async-start(bf16[16,16,1024]{2,0,1:T(8,128)(2,1)} %bitcast.38), calls=%async_computation.3 | async-start | bytes 1048576 | tf_op jit(solution)/shard_map/all_to_all | solution.py:48
  132.1 470.7 %all-gather.6.cloned.1.call-start = ((), (), s32[]{:S(2)}) async-start(), calls=%async_computation.5 | async-start | bytes 67633152 | tf_op jit(solution)/shard_map/all_gather | solution.py:17
  133.2 95.8 %copy-start.2 = (f32[128,512]{1,0:T(8,128)}, f32[128,512]{1,0:T(8,128)S(1)}, u32[]{:S(2)}) copy-start(f32[128,512]{1,0:T(8,128)S(1)} %get-tuple-element.12) | copy-start | bytes 786436
Sparse Core Ops, SparseCore 0:
  124.5 95.8 all-gather.3
  222.1 380.7 all-gather.5
